TPU v7x, 32 devices: a whole 2x2x4 slice. The times are simulated.
32 devices in a mesh: batch: 4 (over z), seq: 8 (over y, x, core).
Axes of the slice: x: 2, y: 2, z: 4, core: 2. Of those that a mesh axis runs over, the one named last changes fastest.
Arguments:
- inputs: bfloat16 [4, 2048, 2048], P('batch', 'seq'), may hold values from -6 to 6
- segment_ids: int32 [4, 2048], P('batch'), may hold values from 0 to 3, never falling along the last dimension, each value on 1 to 1024 neighbouring positions
- w_qkv: bfloat16 [6144, 2048], P('seq'), may hold values from -0.125 to 0.125
- w_out: bfloat16 [2048, 2048], P('seq'), may hold values from -0.125 to 0.125
- w_up: bfloat16 [8192, 2048], P('seq'), may hold values from -0.125 to 0.125
- w_down: bfloat16 [2048, 8192], P('seq'), may hold values from -0.0625 to 0.0625
- gain_attn: float32 [2048], replicated, may hold values from 0.5 to 1.5
- gain_mix: float32 [2048], replicated, may hold values from 0.5 to 1.5
- gain_ffn: float32 [2048], replicated, may hold values from 0.5 to 1.5
- gain_hidden: float32 [8192], replicated, may hold values from 0.5 to 1.5
- cotangent: bfloat16 [4, 2048, 2048], P('batch', 'seq'), may hold values from -6 to 6
Outputs:
- outputs: bfloat16 [4, 2048, 2048], P('batch', 'seq')
- grad_inputs: float32 [4, 2048, 2048], P('batch', 'seq')
- grad_w_qkv: float32 [6144, 2048], P('seq')
- grad_w_out: float32 [2048, 2048], P('seq')
- grad_w_up: float32 [8192, 2048], P('seq')
- grad_w_down: float32 [2048, 8192], P('seq')
- grad_gain_attn: float32 [2048], replicated
- grad_gain_mix: float32 [2048], replicated
- grad_gain_ffn: float32 [2048], replicated
- grad_gain_hidden: float32 [8192], replicated
Inputs may be any that keep to these rules, and one draw needn't show every extreme that they name: `segment_ids`: along a row the ids never fall and each id from 0 to 3 marks one document of 1 to 1024 tokens.
All inputs are finite; a program needn't handle non-finite values.
Results may differ from a plain program's by a relative error of at most 0.02.
Values may be sent and summed in bfloat16 or wider, within the bound.
A program may use at most 448 MiB of HBM per device.

v0:
```python
import math
import jax
import jax.numpy as jnp
from jax import lax
from jax.sharding import PartitionSpec as P

HEADS = 32
HEAD_DIM = 64
LENGTH = 2048
QBLOCK = 512
XBASE = 512
EPSILON = 1e-05
MASKED = -1e30


def norm_rows(values, gain):
    average = jnp.mean(values, axis=-1, keepdims=True)
    centered = values - average
    spread = jnp.mean(centered * centered, axis=-1, keepdims=True)
    return centered * lax.rsqrt(spread + EPSILON) * gain


def gelu_norm(upper, gain):
    return norm_rows(jax.nn.gelu(upper, approximate=False), gain)


def doc_positions(seg_row):
    index = jnp.arange(seg_row.shape[0], dtype=jnp.int32)
    change = jnp.concatenate([jnp.ones((1,), dtype=bool), seg_row[1:] != seg_row[:-1]])
    starts = jnp.where(change, index, jnp.zeros_like(index))
    return index - lax.cummax(starts, axis=0)


def xpos_tables(positions):
    half_dim = HEAD_DIM // 2
    channel = jnp.arange(half_dim, dtype=jnp.float32)
    inverse = jnp.exp(channel * (-math.log(10000.0) / half_dim))
    zeta = (channel * (2.0 / HEAD_DIM) + 0.4) / 1.4
    place = positions.astype(jnp.float32)[..., None]
    angle = place * inverse
    growth = jnp.exp((place - 0.5 * LENGTH) * (1.0 / XBASE) * jnp.log(zeta))
    return (jnp.cos(angle), jnp.sin(angle), growth)


def rotate(values, cosine, sine, growth):
    half_dim = values.shape[-1] // 2
    first = values[..., :half_dim]
    second = values[..., half_dim:]
    cosine = cosine[..., None, :]
    sine = sine[..., None, :]
    growth = growth[..., None, :]
    return jnp.concatenate(
        [(first * cosine - second * sine) * growth, (second * cosine + first * sine) * growth],
        axis=-1,
    )


def allowed_pairs(seg_row, start, count):
    seg_block = lax.dynamic_slice_in_dim(seg_row, start, count, 0)
    query_place = start + jnp.arange(count, dtype=jnp.int32)
    key_place = jnp.arange(seg_row.shape[0], dtype=jnp.int32)
    return (seg_block[:, None] == seg_row[None, :]) & (key_place[None, :] <= query_place[:, None])


def block_scores(query_block, keys, allowed):
    scores = jnp.einsum(
        "qhd,khd->hqk", query_block, keys, preferred_element_type=jnp.float32
    ) * HEAD_DIM ** (-0.5)
    return jnp.where(allowed[None], scores, MASKED)


def attend_row(pieces):
    packed, seg_row = pieces
    query = packed[:, 0]
    keys = packed[:, 1]
    values = packed[:, 2]

    def one_block(start):
        allowed = allowed_pairs(seg_row, start, QBLOCK)
        query_block = lax.dynamic_slice_in_dim(query, start, QBLOCK, 0)
        scores = block_scores(query_block, keys, allowed)
        peak = jnp.max(scores, axis=-1, keepdims=True)
        expo = jnp.exp(scores - peak)
        total = jnp.sum(expo, axis=-1, keepdims=True)
        weights = (expo / total).astype(jnp.bfloat16)
        mixed = jnp.einsum("hqk,khd->qhd", weights, values, preferred_element_type=jnp.float32)
        return (mixed, (peak + jnp.log(total))[..., 0])

    starts = jnp.arange(packed.shape[0] // QBLOCK, dtype=jnp.int32) * QBLOCK
    mixed, logsum = lax.map(one_block, starts)
    return (mixed.reshape(keys.shape), logsum)


def attend_row_back(pieces):
    packed, logsum, grad_row, seg_row = pieces
    query = packed[:, 0]
    keys = packed[:, 1]
    values = packed[:, 2]
    factor = HEAD_DIM ** (-0.5)

    def one_block(carry, block_inputs):
        grad_keys, grad_values = carry
        start, lse_block = block_inputs
        allowed = allowed_pairs(seg_row, start, QBLOCK)
        query_block = lax.dynamic_slice_in_dim(query, start, QBLOCK, 0)
        grad_block = lax.dynamic_slice_in_dim(grad_row, start, QBLOCK, 0)
        scores = block_scores(query_block, keys, allowed)
        weights = jnp.exp(scores - lse_block[..., None])
        grad_weights = jnp.einsum(
            "qhd,khd->hqk", grad_block, values, preferred_element_type=jnp.float32
        )
        inner = jnp.sum(weights * grad_weights, axis=-1, keepdims=True)
        grad_scores = (weights * (grad_weights - inner)).astype(jnp.bfloat16)
        grad_query = (
            jnp.einsum("hqk,khd->qhd", grad_scores, keys, preferred_element_type=jnp.float32)
            * factor
        )
        grad_keys = (
            grad_keys
            + jnp.einsum(
                "hqk,qhd->khd", grad_scores, query_block, preferred_element_type=jnp.float32
            )
            * factor
        )
        grad_values = grad_values + jnp.einsum(
            "hqk,qhd->khd",
            weights.astype(jnp.bfloat16),
            grad_block,
            preferred_element_type=jnp.float32,
        )
        return ((grad_keys, grad_values), grad_query)

    starts = jnp.arange(packed.shape[0] // QBLOCK, dtype=jnp.int32) * QBLOCK
    zeros = jnp.zeros(keys.shape, jnp.float32)
    (grad_keys, grad_values), grad_query = lax.scan(one_block, (zeros, zeros), (starts, logsum))
    grad_query = grad_query.reshape(keys.shape)
    return jnp.stack([grad_query, grad_keys, grad_values], axis=1).astype(jnp.bfloat16)


def times_rows(activations, matrix):
    return lax.dot_general(
        activations,
        matrix,
        (((activations.ndim - 1,), (1,)), ((), ())),
        preferred_element_type=jnp.float32,
    )


def times_matrix(activations, matrix):
    return lax.dot_general(
        activations,
        matrix,
        (((activations.ndim - 1,), (0,)), ((), ())),
        preferred_element_type=jnp.float32,
    )


def weight_term(grads, activations):
    return jnp.einsum("rpe,rpd->ed", grads, activations, preferred_element_type=jnp.float32)


def body(
    inputs,
    segment_ids,
    w_qkv,
    w_out,
    w_up,
    w_down,
    gain_attn,
    gain_mix,
    gain_ffn,
    gain_hidden,
    cotangent,
):
    rows, local, width = inputs.shape
    groups = lax.axis_size("seq")
    length = local * groups
    heads_here = HEADS // groups
    group_width = heads_here * HEAD_DIM
    all_full = (
        lax.all_gather(w_qkv, "seq", axis=0, tiled=True),
        lax.all_gather(w_out, "seq", axis=0, tiled=True),
        lax.all_gather(w_up, "seq", axis=0, tiled=True),
        lax.all_gather(w_down, "seq", axis=0, tiled=True),
    )
    full_positions = jax.vmap(doc_positions)(segment_ids)
    positions = lax.dynamic_slice_in_dim(full_positions, lax.axis_index("seq") * local, local, 1)
    cosine, sine, growth = xpos_tables(positions)
    inputs_f32 = inputs.astype(jnp.float32)
    normed_f32, attn_pull = jax.vjp(norm_rows, inputs_f32, gain_attn)
    normed = normed_f32.astype(jnp.bfloat16)
    qkv = times_rows(normed, all_full[0]).reshape(rows, local, 3, HEADS, HEAD_DIM)
    query, query_pull = jax.vjp(lambda part: rotate(part, cosine, sine, growth), qkv[:, :, 0])
    keys, keys_pull = jax.vjp(lambda part: rotate(part, cosine, sine, 1.0 / growth), qkv[:, :, 1])
    stacked = jnp.stack([query, keys, qkv[:, :, 2]], axis=2).astype(jnp.bfloat16)
    stacked = stacked.reshape(rows, local, 3, groups, group_width)
    gathered = lax.all_to_all(stacked, "seq", split_axis=3, concat_axis=1, tiled=True)
    head_view = gathered.reshape(rows, length, 3, heads_here, HEAD_DIM)
    attended_heads, logsum = lax.map(attend_row, (head_view, segment_ids))
    attended_low = attended_heads.astype(jnp.bfloat16).reshape(rows, length, 1, group_width)
    returned = lax.all_to_all(attended_low, "seq", split_axis=1, concat_axis=2, tiled=True)
    attended = returned.reshape(rows, local, width).astype(jnp.float32)
    mix_f32, mix_pull = jax.vjp(norm_rows, attended, gain_mix)
    mix_in = mix_f32.astype(jnp.bfloat16)
    middle = inputs_f32 + times_rows(mix_in, all_full[1])
    ffn_f32, ffn_pull = jax.vjp(norm_rows, middle, gain_ffn)
    ffn_in = ffn_f32.astype(jnp.bfloat16)
    upper = times_rows(ffn_in, all_full[2])
    hidden_f32, hidden_pull = jax.vjp(gelu_norm, upper, gain_hidden)
    hidden = hidden_f32.astype(jnp.bfloat16)
    outputs = (middle + times_rows(hidden, all_full[3])).astype(jnp.bfloat16)
    back_full = (
        lax.all_gather(w_qkv, "seq", axis=0, tiled=True),
        lax.all_gather(w_out, "seq", axis=0, tiled=True),
        lax.all_gather(w_up, "seq", axis=0, tiled=True),
        lax.all_gather(w_down, "seq", axis=0, tiled=True),
    )
    grad_hidden_in = times_matrix(cotangent, back_full[3])
    grad_upper_f32, grad_gain_hidden = hidden_pull(grad_hidden_in)
    grad_upper = grad_upper_f32.astype(jnp.bfloat16)
    grad_ffn_in = times_matrix(grad_upper, back_full[2])
    grad_middle_part, grad_gain_ffn = ffn_pull(grad_ffn_in)
    grad_middle = cotangent.astype(jnp.float32) + grad_middle_part
    grad_branch = grad_middle.astype(jnp.bfloat16)
    grad_mix_in = times_matrix(grad_branch, back_full[1])
    grad_attended_f32, grad_gain_mix = mix_pull(grad_mix_in)
    grad_attended = grad_attended_f32.astype(jnp.bfloat16).reshape(rows, local, groups, group_width)
    grad_heads_view = lax.all_to_all(grad_attended, "seq", split_axis=2, concat_axis=1, tiled=True)
    grad_heads_view = grad_heads_view.reshape(rows, length, heads_here, HEAD_DIM)
    grad_packed = lax.map(attend_row_back, (head_view, logsum, grad_heads_view, segment_ids))
    grad_packed = grad_packed.reshape(rows, length, 3, 1, group_width)
    grad_local = lax.all_to_all(grad_packed, "seq", split_axis=1, concat_axis=3, tiled=True)
    grad_local = grad_local.reshape(rows, local, 3, HEADS, HEAD_DIM).astype(jnp.float32)
    grad_query_pre = query_pull(grad_local[:, :, 0])[0]
    grad_keys_pre = keys_pull(grad_local[:, :, 1])[0]
    grad_qkv = jnp.stack([grad_query_pre, grad_keys_pre, grad_local[:, :, 2]], axis=2)
    grad_qkv = grad_qkv.reshape(rows, local, 3 * width).astype(jnp.bfloat16)
    grad_normed = times_matrix(grad_qkv, back_full[0])
    grad_input_part, grad_gain_attn = attn_pull(grad_normed)
    grad_inputs = grad_middle + grad_input_part
    grad_w_down = lax.psum_scatter(
        weight_term(cotangent, hidden).astype(jnp.bfloat16), "seq", scatter_dimension=0, tiled=True
    ).astype(jnp.float32)
    grad_w_up = lax.psum_scatter(
        weight_term(grad_upper, ffn_in).astype(jnp.bfloat16), "seq", scatter_dimension=0, tiled=True
    ).astype(jnp.float32)
    grad_w_out = lax.psum_scatter(
        weight_term(grad_branch, mix_in).astype(jnp.bfloat16),
        "seq",
        scatter_dimension=0,
        tiled=True,
    ).astype(jnp.float32)
    grad_w_qkv = lax.psum_scatter(
        weight_term(grad_qkv, normed).astype(jnp.bfloat16), "seq", scatter_dimension=0, tiled=True
    ).astype(jnp.float32)
    grad_w_qkv, grad_w_out, grad_w_up, grad_w_down = (
        lax.psum(grad_w_qkv.astype(jnp.bfloat16), "batch").astype(jnp.float32),
        lax.psum(grad_w_out.astype(jnp.bfloat16), "batch").astype(jnp.float32),
        lax.psum(grad_w_up.astype(jnp.bfloat16), "batch").astype(jnp.float32),
        lax.psum(grad_w_down.astype(jnp.bfloat16), "batch").astype(jnp.float32),
    )
    grad_gain_attn, grad_gain_mix, grad_gain_ffn, grad_gain_hidden = lax.psum(
        (grad_gain_attn, grad_gain_mix, grad_gain_ffn, grad_gain_hidden), ("batch", "seq")
    )
    return (
        outputs,
        grad_inputs,
        grad_w_qkv,
        grad_w_out,
        grad_w_up,
        grad_w_down,
        grad_gain_attn,
        grad_gain_mix,
        grad_gain_ffn,
        grad_gain_hidden,
    )


def solution(mesh):
    in_specs = (
        P("batch", "seq", None),
        P("batch", None),
        P("seq", None),
        P("seq", None),
        P("seq", None),
        P("seq", None),
        P(),
        P(),
        P(),
        P(),
        P("batch", "seq", None),
    )
    out_specs = (
        P("batch", "seq", None),
        P("batch", "seq", None),
        P("seq", None),
        P("seq", None),
        P("seq", None),
        P("seq", None),
        P(),
        P(),
        P(),
        P(),
    )
    return jax.shard_map(body, mesh=mesh, in_specs=in_specs, out_specs=out_specs, check_vma=False)
```

profile of v0, /device:TPU:0, one launch (start us, length us, event | category | flops | bytes accessed | tf_op | source)
XLA Modules:
  0.0 2033.4 jit_solution(4240888310886022481)
XLA Ops:
  12.6 125.4 %all-gather.5.cloned.1.call-done = bf16[6144,2048]{1,0:T(8,128)(2,1)} async-done(((bf16[768,2048]{1,0:T(8,128)(2,1)}), bf16[6144,2048]{1,0:T(8,128)(2,1)}) %all-gather.5.cloned.1.call-update) | async-done | bytes 25165840 | tf_op jit(solution)/shard_map/all_gather | solution.py:181
  138.0 14.7 convolution_bitcast_fusion.2
  159.9 60.2 %all-to-all-done = bf16[1,256,3,8,256]{1,4,2,0,3:T(8,128)(2,1)S(1)} async-done(((bf16[1,256,3,8,256]{1,4,2,0,3:T(8,128)(2,1)}), bf16[1,256,3,8,256]{1,4,2,0,3:T(8,128)(2,1)S(1)}, u32[]{:S(2)}, u32[]{:S(2)}) %all-to-all-start) | async-done | bytes 3145760 | tf_op jit(solution)/shard_map/all_to_all | solution.py:197
  233.3 72.1 %while.45 = (s32[]{:T(128)}, bf16[4,512,4,64]{1,3,2,0:T(8,128)(2,1)}, f32[4,4,512]{2,1,0:T(4,128)}, s32[4]{0:T(128)S(1)}, s32[2048]{0:T(1024)S(1)}, /*index=5*/b...) while((s32[]{:T(128)}, ...), condition=%wide.region_7.8_spmd, body=%wide.region_4.7_spmd.sunk | while | flops 1127217664 | bytes 65882348 | solution.py:90
  333.4 30.4 %all_to_all.49 = bf16[8,2,32768]{2,1,0:T(2,128)(2,1)S(1)} all-to-all(bf16[8,2,32768]{2,1,0:T(2,128)(2,1)} %reshape.1112), channel_id=1, replica_groups=mesh['batch'=4,'seq'=8] {'seq'}, dimensions={0} | all-to-all | bytes 2097152 | tf_op jit(solution)/shard_map/all_to_all | solution.py:201
  395.1 34.0 %fusion.87 = (f32[256]{0:T(256)S(1)}, f32[256,8192]{1,0:T(8,128)}, f32[256,8192]{1,0:T(8,128)}, f32[256,8192]{1,0:T(8,128)}) fusion(bf16[8192,2048]{1,0:T(8,128)(2,1)} %all-gather.9.cloned.1.call-done, f32[1,256,2048]{2,1,0:T(8,128)} %copy-done.9, f32[2048]{0:T(1024)S(1)} %copy-done.48, f32[256]{0:T(256)S(1)} %fusion.76, f32[256]{0:T(256)S(1)} %broadcast_multiply_fusion.1), kind=kOutput, calls=%fused_computation.193 | convolution fusion | flops 8728346624 | bytes 60828672 | tf_op jit(solution)/shard_map/dot_general | solution.py:141
  429.2 128.6 %all-gather.11.cloned.1.call-done = bf16[2048,8192]{1,0:T(8,128)(2,1)} async-done(((bf16[256,8192]{1,0:T(8,128)(2,1)}), bf16[2048,8192]{1,0:T(8,128)(2,1)}) %all-gather.11.cloned.1.call-update) | async-done | bytes 33554448 | tf_op jit(solution)/shard_map/all_gather | solution.py:184
  557.7 20.5 %multiply_reduce_fusion.2 = (f32[256]{0:T(256)S(1)}, f32[256]{0:T(256)S(1)}, f32[256,8192]{1,0:T(8,128)}) fusion(f32[256,8192]{1,0:T(8,128)} %get-tuple-element.328, f32[8192]{0:T(1024)S(1)} %copy-done.29, f32[256]{0:T(256)S(1)} %broadcast_multiply_fusion, bf16[2048,8192]{1,0:T(8,128)(2,1)} %all-gather.11.cloned.1.call-done, ...), kind=kOutput, calls=%fused_computation.55 | convolution fusion | flops 8602517504 | bytes 51416064 | tf_op jit(solution)/shard_map/dot_general | solution.py:150
  600.9 18.2 fusion.57
  656.8 246.3 %while.46 = (s32[]{:T(128)}, f32[2048,4,64]{0,2,1:T(8,128)}, f32[2048,4,64]{0,2,1:T(8,128)}, bf16[4,512,4,64]{1,3,2,0:T(8,128)(2,1)}, s32[4]{0:T(128)S(1)}, /*in...) while((s32[]{:T(128)}, f32[2048,4,64]{0,2,1:T(8,128)}, ...), condition=%wide.region_23.24_spmd.clone, body=%wide.region_21.23_spmd.clone.sunk | while | flops 2753165824 | bytes 193538464 | solution.py:135
  684.8 15.7 multiply_convert_fusion.13
  746.4 14.9 multiply_convert_fusion.13
  807.6 14.9 multiply_convert_fusion.13
  868.7 14.9 multiply_convert_fusion.13
  916.6 52.7 %all_to_all.48 = bf16[1,2048,3,1,256]{4,2,3,0,1:T(4,128)(2,1)S(1)} all-to-all(bf16[1,2048,3,1,256]{4,2,3,0,1:T(4,128)(2,1)} %copy.106), channel_id=1, replica_groups=mesh['batch'=4,'seq'=8] {'seq'}, dimensions={1} | all-to-all | bytes 6291456 | tf_op jit(solution)/shard_map/all_to_all | solution.py:232
  987.5 13.8 convolution_convert_fusion.1
  1002.5 26.2 %convert_bitcast_fusion = bf16[2048,8192]{0,1:T(8,128)(2,1)} fusion(bf16[1,256,2048]{2,1,0:T(8,128)(2,1)S(1)} %copy-done.14, f32[256,8192]{1,0:T(8,128)} %get-tuple-element.328, f32[8192]{0:T(1024)S(1)} %copy-done.30, f32[256]{0:T(256)S(1)} %copy-done.45, f32[256]{0:T(256)S(1)} %copy-done.43), kind=kOutput, calls=%fused_computation.47 | convolution fusion | flops 8615100416 | bytes 43026432 | tf_op jit(solution)/shard_map/rpe,rpd->ed/dot_general | solution.py:159
  1030.7 17.3 convolution_convert_fusion
  1048.1 109.3 %reduce-scatter.5.cloned.1.call-done = bf16[768,2048]{1,0:T(8,128)(2,1)} async-done(((bf16[6144,2048]{1,0:T(8,128)(2,1)}), bf16[768,2048]{1,0:T(8,128)(2,1)}) %reduce-scatter.5.cloned.1.call-update) | async-done | bytes 3145744 | tf_op jit(solution)/shard_map/reduce_scatter | solution.py:253
  1157.5 209.3 %reduce-scatter.11.cloned.1.call-done = bf16[256,8192]{0,1:T(8,128)(2,1)} async-done(((bf16[2048,8192]{0,1:T(8,128)(2,1)}), bf16[256,8192]{0,1:T(8,128)(2,1)}) %reduce-scatter.11.cloned.1.call-update) | async-done | bytes 4194320 | tf_op jit(solution)/shard_map/reduce_scatter | solution.py:241
  1366.8 208.8 %reduce-scatter.9.cloned.1.call-done = bf16[1024,2048]{1,0:T(8,128)(2,1)} async-done(((bf16[8192,2048]{1,0:T(8,128)(2,1)}), bf16[1024,2048]{1,0:T(8,128)(2,1)}) %reduce-scatter.9.cloned.1.call-update) | async-done | bytes 4194320 | tf_op jit(solution)/shard_map/reduce_scatter | solution.py:244
  1575.6 18.8 fusion.50
  1608.3 50.4 %all-reduce.4 = (f32[2048]{0:T(1024)}, f32[2048]{0:T(1024)}, f32[2048]{0:T(1024)}, f32[8192]{0:T(1024)}) all-reduce(f32[2048]{0:T(1024)S(1)} %get-tuple-element.275, f32[2048]{0:T(1024)S(1)} %copy-done.62, f32[2048]{0:T(1024)S(1)} %copy-done.61, f32[8192]{0:T(1024)S(1)} %copy-done.41), channel_id=1, replica_groups=mesh['batch'=4,'seq'=8] {'batch','seq'}, use_global_device_ids=true, to_apply=%region_35.36 | all-reduce | flops 14336 | bytes 114688 | tf_op jit(solution)/shard_map/psum | solution.py:262
  1662.8 345.2 %all-reduce.8.cloned.1.call-done = (bf16[256,8192]{0,1:T(8,128)(2,1)}, bf16[768,2048]{1,0:T(8,128)(2,1)}, bf16[256,2048]{1,0:T(8,128)(2,1)}, bf16[1024,2048]{1,0:T(8,128)(2,1)}) async-done(((bf16[256,8192]{0,1:T(8,128)(2,1)}, bf16[768,2048]{1,0:T(8,128)(2,1)}, bf16[256,2048]{1,0:T(8,128)(2,1)}, bf16[1024,2048]{1,0:T(8,128)(2,1)}), (bf16[256,8192]{0,1:T(8,128)(2,1)}, bf16[768,2048]{1,0:T(8,128)(2,1)}, ...) | async-done | bytes 12582928 | tf_op jit(solution)/shard_map/psum | solution.py:260
  (384 shorter events, 457.9 us)
Async XLA Ops:
  7.2 130.8 %all-gather.5.cloned.1.call-start = ((), (), s32[]{:S(2)}) async-start(), calls=%async_computation.8 | async-start | bytes 28311552 | tf_op jit(solution)/shard_map/all_gather | solution.py:181
  7.9 368.3 %all-gather.7.cloned.1.call-start = ((), (), s32[]{:S(2)}) async-start(), calls=%async_computation.9 | async-start | bytes 9437184 | tf_op jit(solution)/shard_map/all_gather | solution.py:182
  8.7 386.4 %all-gather.9.cloned.1.call-start = ((), (), s32[]{:S(2)}) async-start(), calls=%async_computation.10 | async-start | bytes 37748736 | tf_op jit(solution)/shard_map/all_gather | solution.py:183
  9.4 128.5 %copy-start.39 = (f32[2048]{0:T(1024)S(1)}, f32[2048]{0:T(1024)}, u32[]{:S(2)}) copy-start(f32[2048]{0:T(1024)} %param.21) | copy-start | bytes 24580
  9.4 548.3 %all-gather.11.cloned.1.call-start = ((), (), s32[]{:S(2)}) async-start(), calls=%async_computation.11 | async-start | bytes 37748736 | tf_op jit(solution)/shard_map/all_gather | solution.py:184
  11.2 141.4 %copy-start.46 = (f32[256]{0:T(256)}, f32[256]{0:T(256)S(1)}, u32[]{:S(2)}) copy-start(f32[256]{0:T(256)S(1)} %broadcast_multiply_fusion.3) | copy-start | bytes 3076
  11.7 140.9 %copy-start.51 = (f32[256]{0:T(256)}, f32[256]{0:T(256)S(1)}, u32[]{:S(2)}) copy-start(f32[256]{0:T(256)S(1)} %fusion.74) | copy-start | bytes 3076
  12.5 140.6 %copy-start.31 = (f32[256,32]{0,1:T(8,128)}, f32[256,32]{0,1:T(8,128)S(1)}, u32[]{:S(2)}) copy-start(f32[256,32]{0,1:T(8,128)S(1)} %get-tuple-element.355) | copy-start | bytes 98308
  12.5 140.6 %copy-start.33 = (f32[256,32]{0,1:T(8,128)}, f32[256,32]{0,1:T(8,128)S(1)}, u32[]{:S(2)}) copy-start(f32[256,32]{0,1:T(8,128)S(1)} %get-tuple-element.356) | copy-start | bytes 98308
  12.6 140.5 %copy-start.35 = (f32[256,32]{0,1:T(8,128)}, f32[256,32]{0,1:T(8,128)S(1)}, u32[]{:S(2)}) copy-start(f32[256,32]{0,1:T(8,128)S(1)} %get-tuple-element.353) | copy-start | bytes 98308
  12.6 140.5 %copy-start.37 = (f32[256,32]{0,1:T(8,128)}, f32[256,32]{0,1:T(8,128)S(1)}, u32[]{:S(2)}) copy-start(f32[256,32]{0,1:T(8,128)S(1)} %get-tuple-element.354) | copy-start | bytes 98308
  156.0 64.1 %all-to-all-start = ((bf16[1,256,3,8,256]{1,4,2,0,3:T(8,128)(2,1)}), bf16[1,256,3,8,256]{1,4,2,0,3:T(8,128)(2,1)S(1)}, u32[]{:S(2)}, u32[]{:S(2)}) async-start(bf16[1,256,3,8,256]{1,4,2,0,3:T(8,128)(2,1)} %pad_maximum_fusion), calls=%async_computation | async-start | bytes 6291456 | tf_op jit(solution)/shard_map/all_to_all | solution.py:197
  382.8 236.3 %copy-start.53 = (f32[256]{0:T(256)}, f32[256]{0:T(256)S(1)}, u32[]{:S(2)}) copy-start(f32[256]{0:T(256)S(1)} %broadcast_multiply_fusion.1) | copy-start | bytes 3076
  384.4 234.7 %copy-start.55 = (f32[256]{0:T(256)}, f32[256]{0:T(256)S(1)}, u32[]{:S(2)}) copy-start(f32[256]{0:T(256)S(1)} %fusion.76) | copy-start | bytes 3076
  384.4 173.3 %copy-start.13 = (bf16[1,256,2048]{2,1,0:T(8,128)(2,1)S(1)}, bf16[1,256,2048]{2,1,0:T(8,128)(2,1)}, u32[]{:S(2)}) copy-start(bf16[1,256,2048]{2,1,0:T(8,128)(2,1)} %param.25) | copy-start | bytes 3145732
  384.5 173.3 %copy-start.29 = (f32[8192]{0:T(1024)S(1)}, f32[8192]{0:T(1024)}, u32[]{:S(2)}) copy-start(f32[8192]{0:T(1024)} %param.24) | copy-start | bytes 98308
  429.2 159.1 %copy-start.42 = (f32[256]{0:T(256)}, f32[256]{0:T(256)S(1)}, u32[]{:S(2)}) copy-start(f32[256]{0:T(256)S(1)} %broadcast_multiply_fusion) | copy-start | bytes 3076
  632.7 19.8 all-to-all-start.2
  637.0 411.1 %reduce-scatter.7.cloned.1.call-start = ((), (), s32[]{:S(2)}) async-start(), calls=%async_computation.13 | async-start | bytes 9437184 | tf_op jit(solution)/shard_map/reduce_scatter | solution.py:247
  645.9 511.5 %reduce-scatter.5.cloned.1.call-start = ((), (), s32[]{:S(2)}) async-start(), calls=%async_computation.12 | async-start | bytes 28311552 | tf_op jit(solution)/shard_map/reduce_scatter | solution.py:253
  1001.3 365.5 %reduce-scatter.11.cloned.1.call-start = ((), (), s32[]{:S(2)}) async-start(), calls=%async_computation.15 | async-start | bytes 37748736 | tf_op jit(solution)/shard_map/reduce_scatter | solution.py:241
  1028.7 546.9 %reduce-scatter.9.cloned.1.call-start = ((), (), s32[]{:S(2)}) async-start(), calls=%async_computation.14 | async-start | bytes 37748736 | tf_op jit(solution)/shard_map/reduce_scatter | solution.py:244
  1048.1 959.9 %all-reduce.8.cloned.1.call-start = ((), (), s32[]{:S(2)}) async-start(), calls=%async_computation.16 | async-start | bytes 25165824 | tf_op jit(solution)/shard_map/psum | solution.py:260
  1594.5 64.2 %copy-start.58 = (f32[256]{0:T(256)S(1)}, f32[256]{0:T(256)}, u32[]{:S(2)}) copy-start(f32[256]{0:T(256)} %copy-done.57) | copy-start | bytes 3076
  (80 other events, 557.0 us)
Sparse Core Ops, SparseCore 0:
  9.9 128.0 all-gather.4
  139.8 76.6 all-gather.6
  218.4 176.6 all-gather.8
  396.9 160.8 all-gather.10
  646.0 72.5 reduce-scatter.6
  1001.4 156.0 reduce-scatter.4
  1161.5 205.2 reduce-scatter.10
  1370.3 205.2 reduce-scatter.8
  1578.8 429.1 all-reduce.7
where the time goes:
time: 2040 us; the launch traced here: 2030 us
  waiting for transfers between devices  1210 us (59%)
  matrix products  389 us (19%)
  other arithmetic  176 us (9%)
  blocking collectives  133 us (7%)
  local copies, waits for them, and re-layouts  88.6 us (4%)
    psum x1, waiting for transfers between devices, body(): lax.psum(grad_w_down.astype(jnp.bfloat16), 'batch').astype(jnp.float32)  345 us
    reduce_scatter x1, waiting for transfers between devices, body(): lax.psum_scatter(weight_term(cotangent, hidden).astype(jnp.bfloat16), 'se...  209 us
    reduce_scatter x1, waiting for transfers between devices, body(): lax.psum_scatter(weight_term(grad_upper, ffn_in).astype(jnp.bfloat16), 's...  209 us
    all_gather x1, waiting for transfers between devices, body(): lax.all_gather(w_down, 'seq', axis=0, tiled=True)  129 us
    all_gather x1, waiting for transfers between devices, body(): lax.all_gather(w_qkv, 'seq', axis=0, tiled=True)  125 us
    reduce_scatter x1, waiting for transfers between devices, body(): lax.psum_scatter(weight_term(grad_qkv, normed).astype(jnp.bfloat16), 'seq...  109 us
    dot_general x4, matrix products, times_rows(): lax.dot_general(activations, matrix, (((activations.ndim - 1,), (1,)), ((...  74 us
    dot_general x4, matrix products, weight_term(): jnp.einsum('rpe,rpd->ed', grads, activations, preferred_element_type=jnp....  63.1 us
  transfers between devices with their start and end apart: 11, of which 9 were waited for; matrix products, arithmetic and copies ran while one was open for 27% of the time, Pallas kernels for 0%

commit v1 on v0

--- a/solution.py
+++ b/solution.py
@@ -11,6 +11,19 @@
 XBASE = 512
 EPSILON = 1e-05
 MASKED = -1e30
+
+
+def collect(x, axis, dim):
+    ways = lax.axis_size(axis)
+    up = [(d, (d + 1) % ways) for d in range(ways)]
+    down = [(d, (d - 1) % ways) for d in range(ways)]
+    earlier, later = ([x], [x])
+    for _ in range(ways // 2):
+        earlier.append(lax.ppermute(earlier[-1], axis, up))
+    for _ in range((ways - 1) // 2):
+        later.append(lax.ppermute(later[-1], axis, down))
+    line = jnp.concatenate([*earlier[::-1], *later[1:]], axis=dim)
+    return jnp.roll(line, (lax.axis_index(axis) - ways // 2) * x.shape[dim], axis=dim)
 
 
 def norm_rows(values, gain):
@@ -178,7 +191,7 @@
     heads_here = HEADS // groups
     group_width = heads_here * HEAD_DIM
     all_full = (
-        lax.all_gather(w_qkv, "seq", axis=0, tiled=True),
+        collect(w_qkv, "seq", 0),
         lax.all_gather(w_out, "seq", axis=0, tiled=True),
         lax.all_gather(w_up, "seq", axis=0, tiled=True),
         lax.all_gather(w_down, "seq", axis=0, tiled=True),

time: 2040 us -> 2420 us (1.19)
  waiting for transfers between devices: 1210 us -> 1480 us
  local copies, waits for them, and re-layouts: 88.6 us -> 170 us
    ppermute x0 -> x7, waiting for transfers between devices: none -> 424 us  [the longest x4 424 us: collect(): earlier.append(lax.ppermute(earlier[-1], axis, up))]
    all_gather x1, waiting for transfers between devices: 129 us -> 0.02 us  [body(): lax.all_gather(w_down, 'seq', axis=0, tiled=True)]
    unnamed x128 -> x145, local copies, waits for them, and re-layouts: 21.6 us -> 76.9 us
  transfers between devices with their start and end apart: 11 -> 18, of which waited for: 9 -> 11; matrix products, arithmetic and copies ran while one was open for 27% -> 27% of each run, Pallas kernels for 0% -> 0%
where the time goes in v1:
time: 2420 us; the launch traced here: 2410 us
  waiting for transfers between devices  1480 us (61%)
  matrix products  411 us (17%)
  other arithmetic  174 us (7%)
  local copies, waits for them, and re-layouts  170 us (7%)
  blocking collectives  118 us (5%)
  starting transfers between devices  30.2 us (1%)
    ppermute x4, waiting for transfers between devices, collect(): earlier.append(lax.ppermute(earlier[-1], axis, up))  424 us
    psum x1, waiting for transfers between devices, body(): lax.psum(grad_w_down.astype(jnp.bfloat16), 'batch').astype(jnp.float32)  369 us
    reduce_scatter x1, waiting for transfers between devices, body(): lax.psum_scatter(weight_term(grad_upper, ffn_in).astype(jnp.bfloat16), 's...  209 us
    reduce_scatter x1, waiting for transfers between devices, body(): lax.psum_scatter(weight_term(cotangent, hidden).astype(jnp.bfloat16), 'se...  209 us
    reduce_scatter x1, waiting for transfers between devices, body(): lax.psum_scatter(weight_term(grad_qkv, normed).astype(jnp.bfloat16), 'seq...  110 us
    all_gather x1, waiting for transfers between devices, body(): lax.all_gather(w_qkv, 'seq', axis=0, tiled=True)  107 us
    unnamed x145, local copies, waits for them, and re-layouts  76.9 us
    dot_general x4, matrix products, times_rows(): lax.dot_general(activations, matrix, (((activations.ndim - 1,), (1,)), ((...  75.9 us
  transfers between devices with their start and end apart: 18, of which 11 were waited for; matrix products, arithmetic and copies ran while one was open for 27% of the time, Pallas kernels for 0%

profile of v1, /device:TPU:0, one launch (start us, length us, event | category | flops | bytes accessed | tf_op | source)
XLA Modules:
  0.0 2413.0 jit_solution(7680290690394493305)
XLA Ops:
  9.9 70.3 %collective-permute-done = bf16[768,2048]{1,0:T(8,128)(2,1)S(1)} collective-permute-done((bf16[768,2048]{1,0:T(8,128)(2,1)}, bf16[768,2048]{1,0:T(8,128)(2,1)S(1)}, u32[]{:S(2)}, u32[]{:S(2)}) %collective-permute-start) | collective-permute-done | bytes 3145760 | tf_op jit(solution)/shard_map/ppermute | solution.py:22
  84.5 110.1 %collective-permute-done.1 = bf16[768,2048]{1,0:T(8,128)(2,1)S(1)} collective-permute-done((bf16[768,2048]{1,0:T(8,128)(2,1)S(1)}, bf16[768,2048]{1,0:T(8,128)(2,1)S(1)}, u32[]{:S(2)}, u32[]{:S(2)}) %collective-permute-start.1) | collective-permute-done | bytes 3145760 | tf_op jit(solution)/shard_map/ppermute | solution.py:22
  203.2 131.2 %collective-permute-done.2 = bf16[768,2048]{1,0:T(8,128)(2,1)} collective-permute-done((bf16[768,2048]{1,0:T(8,128)(2,1)S(1)}, bf16[768,2048]{1,0:T(8,128)(2,1)}, u32[]{:S(2)}, u32[]{:S(2)}) %collective-permute-start.2) | collective-permute-done | bytes 3145760 | tf_op jit(solution)/shard_map/ppermute | solution.py:22
  342.3 111.9 %collective-permute-done.3 = bf16[768,2048]{1,0:T(8,128)(2,1)} collective-permute-done((bf16[768,2048]{1,0:T(8,128)(2,1)}, bf16[768,2048]{1,0:T(8,128)(2,1)}, u32[]{:S(2)}, u32[]{:S(2)}) %collective-permute-start.3) | collective-permute-done | bytes 3145760 | tf_op jit(solution)/shard_map/ppermute | solution.py:22
  508.8 22.5 constant_dynamic-slice_fusion
  559.8 41.9 %all-to-all-done = bf16[1,256,3,8,256]{1,4,2,0,3:T(8,128)(2,1)S(1)} async-done(((bf16[1,256,3,8,256]{1,4,2,0,3:T(8,128)(2,1)}), bf16[1,256,3,8,256]{1,4,2,0,3:T(8,128)(2,1)S(1)}, u32[]{:S(2)}, u32[]{:S(2)}) %all-to-all-start) | async-done | bytes 3145760 | tf_op jit(solution)/shard_map/all_to_all | solution.py:210
  614.1 75.0 %while.45 = (s32[]{:T(128)}, bf16[4,512,4,64]{1,3,2,0:T(8,128)(2,1)}, f32[4,4,512]{2,1,0:T(4,128)}, s32[4]{0:T(128)S(1)}, s32[2048]{0:T(1024)S(1)}, /*index=5*/b...) while((s32[]{:T(128)}, ...), condition=%wide.region_7.8_spmd, body=%wide.region_4.7_spmd.sunk | while | flops 1127217664 | bytes 57494696 | solution.py:103
  716.9 19.8 all_to_all.49
  759.9 34.1 %fusion.87 = (f32[256]{0:T(256)S(1)}, f32[256,8192]{1,0:T(8,128)}, f32[256,8192]{1,0:T(8,128)}, f32[256,8192]{1,0:T(8,128)}) fusion(bf16[8192,2048]{1,0:T(8,128)(2,1)} %all-gather.7.cloned.1.call-done, f32[1,256,2048]{2,1,0:T(8,128)} %copy-done.11, f32[2048]{0:T(1024)S(1)} %copy-done.48, f32[256]{0:T(256)S(1)} %fusion.76, f32[256]{0:T(256)S(1)} %broadcast_multiply_fusion.1), kind=kOutput, calls=%fused_computation.210 | convolution fusion | flops 8728346624 | bytes 60828672 | tf_op jit(solution)/shard_map/dot_general | solution.py:154
  794.1 20.5 multiply_reduce_fusion.2
  837.4 18.1 fusion.57
  892.9 261.8 %while.46 = (s32[]{:T(128)}, f32[2048,4,64]{0,2,1:T(8,128)}, f32[2048,4,64]{0,2,1:T(8,128)}, bf16[4,512,4,64]{1,3,2,0:T(8,128)(2,1)}, s32[4]{0:T(128)S(1)}, /*in...) while((s32[]{:T(128)}, f32[2048,4,64]{0,2,1:T(8,128)}, ...), condition=%wide.region_23.24_spmd.clone, body=%wide.region_21.23_spmd.clone.sunk | while | flops 2753165824 | bytes 185149760 | solution.py:148
  920.8 15.7 multiply_convert_fusion.13
  986.5 14.9 multiply_convert_fusion.13
  1168.2 52.7 %all_to_all.48 = bf16[1,2048,3,1,256]{4,2,3,0,1:T(4,128)(2,1)S(1)} all-to-all(bf16[1,2048,3,1,256]{4,2,3,0,1:T(4,128)(2,1)} %copy.106), channel_id=1, replica_groups=mesh['batch'=4,'seq'=8] {'seq'}, dimensions={1} | all-to-all | bytes 6291456 | tf_op jit(solution)/shard_map/all_to_all | solution.py:245
  1254.5 24.2 %convolution_convert_fusion = bf16[8192,2048]{1,0:T(8,128)(2,1)} fusion(bf16[256,8192]{1,0:T(8,128)(2,1)} %add_convert_fusion, f32[1,256,2048]{2,1,0:T(8,128)S(1)} %copy-done.13, f32[2048]{0:T(1024)S(1)} %copy-done.49, f32[256]{0:T(256)S(1)} %copy-done.56, f32[256]{0:T(256)S(1)} %copy-done.54), kind=kOutput, calls=%fused_computation.48 | convolution fusion | flops 8608808960 | bytes 39856128 | tf_op jit(solution)/shard_map/rpe,rpd->ed/dot_general | solution.py:172
  1279.5 19.4 convert_bitcast_fusion
  1299.7 109.6 %reduce-scatter.5.cloned.1.call-done = bf16[768,2048]{1,0:T(8,128)(2,1)} async-done(((bf16[6144,2048]{1,0:T(8,128)(2,1)}), bf16[768,2048]{1,0:T(8,128)(2,1)}) %reduce-scatter.5.cloned.1.call-update) | async-done | bytes 3145744 | tf_op jit(solution)/shard_map/reduce_scatter | solution.py:266
  1409.3 209.1 %reduce-scatter.9.cloned.1.call-done = bf16[1024,2048]{1,0:T(8,128)(2,1)} async-done(((bf16[8192,2048]{1,0:T(8,128)(2,1)}), bf16[1024,2048]{1,0:T(8,128)(2,1)}) %reduce-scatter.9.cloned.1.call-update) | async-done | bytes 4194320 | tf_op jit(solution)/shard_map/reduce_scatter | solution.py:257
  1618.5 208.9 %reduce-scatter.11.cloned.1.call-done = bf16[256,8192]{0,1:T(8,128)(2,1)} async-done(((bf16[2048,8192]{0,1:T(8,128)(2,1)}), bf16[256,8192]{0,1:T(8,128)(2,1)}) %reduce-scatter.11.cloned.1.call-update) | async-done | bytes 4194320 | tf_op jit(solution)/shard_map/reduce_scatter | solution.py:254
  1827.4 20.4 fusion.50
  1847.8 106.9 %all-gather.11.cloned.1.call-done = bf16[6144,2048]{1,0:T(8,128)(2,1)} async-done(((bf16[768,2048]{1,0:T(8,128)(2,1)}), bf16[6144,2048]{1,0:T(8,128)(2,1)}) %all-gather.11.cloned.1.call-update) | async-done | bytes 25165840 | tf_op jit(solution)/shard_map/all_gather | solution.py:226
  1968.9 45.4 %all-reduce.4 = (f32[2048]{0:T(1024)}, f32[2048]{0:T(1024)}, f32[2048]{0:T(1024)}, f32[8192]{0:T(1024)}) all-reduce(f32[2048]{0:T(1024)S(1)} %get-tuple-element.275, f32[2048]{0:T(1024)S(1)} %copy-done.62, f32[2048]{0:T(1024)S(1)} %copy-done.61, f32[8192]{0:T(1024)S(1)} %copy-done.41), channel_id=1, replica_groups=mesh['batch'=4,'seq'=8] {'batch','seq'}, use_global_device_ids=true, to_apply=%region_35.36 | all-reduce | flops 14336 | bytes 114688 | tf_op jit(solution)/shard_map/psum | solution.py:275
  2018.4 368.7 %all-reduce.8.cloned.1.call-done = (bf16[256,8192]{0,1:T(8,128)(2,1)}, bf16[768,2048]{1,0:T(8,128)(2,1)}, bf16[256,2048]{1,0:T(8,128)(2,1)}, bf16[1024,2048]{1,0:T(8,128)(2,1)}) async-done(((bf16[256,8192]{0,1:T(8,128)(2,1)}, bf16[768,2048]{1,0:T(8,128)(2,1)}, bf16[256,2048]{1,0:T(8,128)(2,1)}, bf16[1024,2048]{1,0:T(8,128)(2,1)}), (bf16[256,8192]{0,1:T(8,128)(2,1)}, bf16[768,2048]{1,0:T(8,128)(2,1)}, ...) | async-done | bytes 12582928 | tf_op jit(solution)/shard_map/psum | solution.py:273
  (372 shorter events, 605.3 us)
Async XLA Ops:
  7.2 330.7 %copy-start.26 = (s32[1,2048]{1,0:T(1,128)S(1)}, s32[1,2048]{1,0:T(1,128)}, u32[]{:S(2)}) copy-start(s32[1,2048]{1,0:T(1,128)} %param.16) | copy-start | bytes 24580
  7.2 331.6 %copy-start.4 = (bf16[1,256,2048]{2,1,0:T(8,128)(2,1)S(1)}, bf16[1,256,2048]{2,1,0:T(8,128)(2,1)}, u32[]{:S(2)}) copy-start(bf16[1,256,2048]{2,1,0:T(8,128)(2,1)} %param.15) | copy-start | bytes 3145732
  7.2 744.4 %all-gather.5.cloned.1.call-start = ((), (), s32[]{:S(2)}) async-start(), calls=%async_computation.8 | async-start | bytes 9437184 | tf_op jit(solution)/shard_map/all_gather | solution.py:195
  7.9 752.0 %all-gather.7.cloned.1.call-start = ((), (), s32[]{:S(2)}) async-start(), calls=%async_computation.9 | async-start | bytes 37748736 | tf_op jit(solution)/shard_map/all_gather | solution.py:196
  8.7 785.4 %all-gather.9.cloned.1.call-start = ((), (), s32[]{:S(2)}) async-start(), calls=%async_computation.10 | async-start | bytes 37748736 | tf_op jit(solution)/shard_map/all_gather | solution.py:197
  9.4 70.8 %collective-permute-start = (bf16[768,2048]{1,0:T(8,128)(2,1)}, bf16[768,2048]{1,0:T(8,128)(2,1)S(1)}, u32[]{:S(2)}, u32[]{:S(2)}) collective-permute-start(bf16[768,2048]{1,0:T(8,128)(2,1)} %param.17), channel_id=1, source_target_pairs={{0,1},{1,2},{2,3},{3,4},{4,5},{5,6},{6,7},{7,0},{8,9},{9,10},{10,1... | collective-permute-start | bytes 9437192 | tf_op jit(solution)/shard_map/ppermute | solution.py:22
  81.8 112.8 %collective-permute-start.1 = (bf16[768,2048]{1,0:T(8,128)(2,1)S(1)}, bf16[768,2048]{1,0:T(8,128)(2,1)S(1)}, u32[]{:S(2)}, u32[]{:S(2)}) collective-permute-start(bf16[768,2048]{1,0:T(8,128)(2,1)S(1)} %collective-permute-done), channel_id=1, source_target_pairs={{0,1},{1,2},{2,3},{3,4},{4,5},{5,6},{6,7},{7,0},{8,9},{9,10},{10,1... | collective-permute-start | bytes 9437192 | tf_op jit(solution)/shard_map/ppermute | solution.py:22
  82.4 118.5 %collective-permute-start.4 = (bf16[768,2048]{1,0:T(8,128)(2,1)}, bf16[768,2048]{1,0:T(8,128)(2,1)}, u32[]{:S(2)}, u32[]{:S(2)}) collective-permute-start(bf16[768,2048]{1,0:T(8,128)(2,1)} %param.17), channel_id=1, source_target_pairs={{0,7},{1,0},{2,1},{3,2},{4,3},{5,4},{6,5},{7,6},{8,15},{9,8},{10,9... | collective-permute-start | bytes 9437192 | tf_op jit(solution)/shard_map/ppermute | solution.py:24
  196.7 137.8 %collective-permute-start.2 = (bf16[768,2048]{1,0:T(8,128)(2,1)S(1)}, bf16[768,2048]{1,0:T(8,128)(2,1)}, u32[]{:S(2)}, u32[]{:S(2)}) collective-permute-start(bf16[768,2048]{1,0:T(8,128)(2,1)S(1)} %collective-permute-done.1), channel_id=1, source_target_pairs={{0,1},{1,2},{2,3},{3,4},{4,5},{5,6},{6,7},{7,0},{8,9},{9,10},{10,1... | collective-permute-start | bytes 9437192 | tf_op jit(solution)/shard_map/ppermute | solution.py:22
  200.9 138.5 %collective-permute-start.5 = (bf16[768,2048]{1,0:T(8,128)(2,1)}, bf16[768,2048]{1,0:T(8,128)(2,1)}, u32[]{:S(2)}, u32[]{:S(2)}) collective-permute-start(bf16[768,2048]{1,0:T(8,128)(2,1)} %collective-permute-done.4), channel_id=1, source_target_pairs={{0,7},{1,0},{2,1},{3,2},{4,3},{5,4},{6,5},{7,6},{8,15},{9,8},{10,9... | collective-permute-start | bytes 9437192 | tf_op jit(solution)/shard_map/ppermute | solution.py:24
  334.5 119.8 %collective-permute-start.3 = (bf16[768,2048]{1,0:T(8,128)(2,1)}, bf16[768,2048]{1,0:T(8,128)(2,1)}, u32[]{:S(2)}, u32[]{:S(2)}) collective-permute-start(bf16[768,2048]{1,0:T(8,128)(2,1)} %collective-permute-done.2), channel_id=1, source_target_pairs={{0,1},{1,2},{2,3},{3,4},{4,5},{5,6},{6,7},{7,0},{8,9},{9,10},{10,1... | collective-permute-start | bytes 9437192 | tf_op jit(solution)/shard_map/ppermute | solution.py:22
  339.5 137.5 %collective-permute-start.6 = (bf16[768,2048]{1,0:T(8,128)(2,1)}, bf16[768,2048]{1,0:T(8,128)(2,1)}, u32[]{:S(2)}, u32[]{:S(2)}) collective-permute-start(bf16[768,2048]{1,0:T(8,128)(2,1)} %collective-permute-done.5), channel_id=1, source_target_pairs={{0,7},{1,0},{2,1},{3,2},{4,3},{5,4},{6,5},{7,6},{8,15},{9,8},{10,9... | collective-permute-start | bytes 9437192 | tf_op jit(solution)/shard_map/ppermute | solution.py:24
  342.2 204.5 %copy-start.31 = (f32[256,32]{0,1:T(8,128)}, f32[256,32]{0,1:T(8,128)S(1)}, u32[]{:S(2)}) copy-start(f32[256,32]{0,1:T(8,128)S(1)} %get-tuple-element.355) | copy-start | bytes 98308
  342.2 204.5 %copy-start.33 = (f32[256,32]{0,1:T(8,128)}, f32[256,32]{0,1:T(8,128)S(1)}, u32[]{:S(2)}) copy-start(f32[256,32]{0,1:T(8,128)S(1)} %get-tuple-element.356) | copy-start | bytes 98308
  342.3 204.4 %copy-start.35 = (f32[256,32]{0,1:T(8,128)}, f32[256,32]{0,1:T(8,128)S(1)}, u32[]{:S(2)}) copy-start(f32[256,32]{0,1:T(8,128)S(1)} %get-tuple-element.353) | copy-start | bytes 98308
  342.3 204.4 %copy-start.37 = (f32[256,32]{0,1:T(8,128)}, f32[256,32]{0,1:T(8,128)S(1)}, u32[]{:S(2)}) copy-start(f32[256,32]{0,1:T(8,128)S(1)} %get-tuple-element.354) | copy-start | bytes 98308
  549.6 52.1 %all-to-all-start = ((bf16[1,256,3,8,256]{1,4,2,0,3:T(8,128)(2,1)}), bf16[1,256,3,8,256]{1,4,2,0,3:T(8,128)(2,1)S(1)}, u32[]{:S(2)}, u32[]{:S(2)}) async-start(bf16[1,256,3,8,256]{1,4,2,0,3:T(8,128)(2,1)} %pad_maximum_fusion), calls=%async_computation | async-start | bytes 6291456 | tf_op jit(solution)/shard_map/all_to_all | solution.py:210
  868.9 19.7 all-to-all-start.2
  873.2 426.5 %reduce-scatter.7.cloned.1.call-start = ((), (), s32[]{:S(2)}) async-start(), calls=%async_computation.13 | async-start | bytes 9437184 | tf_op jit(solution)/shard_map/reduce_scatter | solution.py:260
  882.0 527.4 %reduce-scatter.5.cloned.1.call-start = ((), (), s32[]{:S(2)}) async-start(), calls=%async_computation.12 | async-start | bytes 28311552 | tf_op jit(solution)/shard_map/reduce_scatter | solution.py:266
  1252.9 365.6 %reduce-scatter.9.cloned.1.call-start = ((), (), s32[]{:S(2)}) async-start(), calls=%async_computation.14 | async-start | bytes 37748736 | tf_op jit(solution)/shard_map/reduce_scatter | solution.py:257
  1278.7 548.6 %reduce-scatter.11.cloned.1.call-start = ((), (), s32[]{:S(2)}) async-start(), calls=%async_computation.15 | async-start | bytes 37748736 | tf_op jit(solution)/shard_map/reduce_scatter | solution.py:254
  1298.9 655.8 %all-gather.11.cloned.1.call-start = ((), (), s32[]{:S(2)}) async-start(), calls=%async_computation.11 | async-start | bytes 28311552 | tf_op jit(solution)/shard_map/all_gather | solution.py:226
  1299.7 1087.5 %all-reduce.8.cloned.1.call-start = ((), (), s32[]{:S(2)}) async-start(), calls=%async_computation.16 | async-start | bytes 25165824 | tf_op jit(solution)/shard_map/psum | solution.py:273
  (68 other events, 2058.5 us)
Sparse Core Ops, SparseCore 0:
  9.9 73.9 all-gather.4
  85.8 285.4 all-gather.6
  373.2 201.4 all-gather.8
  882.1 72.5 reduce-scatter.6
  1253.0 156.2 reduce-scatter.4
  1413.2 205.2 reduce-scatter.8
  1622.0 205.2 reduce-scatter.10
  1829.4 125.2 all-gather.10
  1957.9 429.1 all-reduce.7
